TPU v7x, 256 devices: a whole 4x4x8 slice. The times are simulated.
256 devices in a mesh: dp: 32 (over y_lo, z, core), ctx: 8 (over y_hi, x).
Axes of the slice: x: 4, y: 4 (y_hi: 2, y_lo: 2; y = y_hi * 2 + y_lo), z: 8, core: 2. Of those that a mesh axis runs over, the one named last changes fastest.
Arguments:
- query_proj: bfloat16 [64, 512, 4096], P('dp', 'ctx'), may hold values from -5 to 5
- key_proj: bfloat16 [64, 512, 1024], P('dp', 'ctx'), may hold values from -5 to 5
- value_proj: bfloat16 [64, 512, 1024], P('dp', 'ctx'), may hold values from -6 to 6
- grad_attn: bfloat16 [64, 512, 4096], P('dp', 'ctx'), may hold values from -6 to 6
- doc_lengths: int32 [64, 8], replicated, may hold values from 1 to 128, 512 in all within a row
- mask_tiles: int32 [64, 8, 8], replicated, may hold values from 0 to 1, as said below
- pair_flags: int32 [32], replicated, may hold values from 0 to 1, as said below
Outputs:
- attn_out: bfloat16 [64, 512, 4096], P('dp', 'ctx')
- grad_query: bfloat16 [64, 512, 4096], P('dp', 'ctx')
- grad_key: bfloat16 [64, 512, 1024], P('dp', 'ctx')
- grad_value: bfloat16 [64, 512, 1024], P('dp', 'ctx')
Inputs may be any that keep to these rules, and one draw needn't show every extreme that they name: `doc_lengths`: each row sums to 512. mask_tiles[n, t, t] = 1 for every sequence n and tile t. pair_flags[r] = pair_flags[r XOR (16)] for every r.
All inputs are finite; a program needn't handle non-finite values.
Results may differ from a plain program's by a relative error of at most 0.03.
Values may be sent and summed in bfloat16 or wider, within the bound.
A program may use at most 128 MiB of HBM per device.

v0:
```python
import jax
import jax.numpy as jnp
from jax import lax
from jax.sharding import PartitionSpec as P

QUERY_HEADS = 32
KEY_VALUE_HEADS = 8
HEAD_SIZE = 128


def from_partner(value, axis, distance):
    mask = 2**distance
    pairs = [(source, source ^ mask) for source in range(lax.axis_size(axis))]
    return lax.ppermute(value, axis, pairs)


def sequence_core(
    query_rows, sequence_keys, sequence_values, sequence_gradients, lengths, tile_table, row_start
):
    rows = query_rows.shape[0]
    length_total = sequence_keys.shape[0]
    groups = sequence_keys.shape[1] // HEAD_SIZE
    group_ratio = QUERY_HEADS // KEY_VALUE_HEADS
    scale = HEAD_SIZE ** (-0.5)
    row_pos = row_start + jnp.arange(rows, dtype=jnp.int32)
    col_pos = jnp.arange(length_total, dtype=jnp.int32)
    ends = jnp.cumsum(lengths)[:-1]
    row_doc = jnp.sum((row_pos[:, None] >= ends[None, :]).astype(jnp.int32), axis=1)
    col_doc = jnp.sum((col_pos[:, None] >= ends[None, :]).astype(jnp.int32), axis=1)
    tile_count = tile_table.shape[0]
    tile_len = length_total // tile_count
    tile_ids = jnp.arange(tile_count, dtype=jnp.int32)
    row_pick = ((row_pos // tile_len)[:, None] == tile_ids[None, :]).astype(jnp.float32)
    col_pick = ((col_pos // tile_len)[:, None] == tile_ids[None, :]).astype(jnp.float32)
    tile_map = jnp.dot(jnp.dot(row_pick, tile_table.astype(jnp.float32)), col_pick.T) > 0.5
    allowed = (
        (col_pos[None, :] <= row_pos[:, None])
        & ((col_doc[None, :] == row_doc[:, None]) | (col_doc[None, :] == 0))
        & tile_map
    )
    heads_of_queries = query_rows.reshape(rows, groups, group_ratio, HEAD_SIZE)
    heads_of_keys = sequence_keys.reshape(length_total, groups, HEAD_SIZE)
    heads_of_values = sequence_values.reshape(length_total, groups, HEAD_SIZE)
    head_gradients = sequence_gradients.reshape(rows, groups, group_ratio, HEAD_SIZE)
    scores = (
        jnp.einsum(
            "igrd,jgd->grij", heads_of_queries, heads_of_keys, preferred_element_type=jnp.float32
        )
        * scale
    )
    scores = jnp.where(allowed, scores, -1e30)
    peak = jnp.max(scores, axis=-1, keepdims=True)
    expd = jnp.where(allowed, jnp.exp(scores - peak), 0.0)
    probs = expd / jnp.sum(expd, axis=-1, keepdims=True)
    probs_b = probs.astype(jnp.bfloat16)
    attn = jnp.einsum(
        "grij,jgd->igrd", probs_b, heads_of_values, preferred_element_type=jnp.float32
    ).astype(jnp.bfloat16)
    delta = jnp.transpose(
        jnp.sum(head_gradients.astype(jnp.float32) * attn.astype(jnp.float32), axis=-1), (1, 2, 0)
    )
    value_gradient = jnp.einsum(
        "grij,igrd->jgd", probs_b, head_gradients, preferred_element_type=jnp.float32
    )
    dprobs = jnp.einsum(
        "igrd,jgd->grij", head_gradients, heads_of_values, preferred_element_type=jnp.float32
    )
    dscores = (probs * (dprobs - delta[..., None]) * scale).astype(jnp.bfloat16)
    grad_q = jnp.einsum(
        "grij,jgd->igrd", dscores, heads_of_keys, preferred_element_type=jnp.float32
    )
    key_gradient = jnp.einsum(
        "grij,igrd->jgd", dscores, heads_of_queries, preferred_element_type=jnp.float32
    )
    return (
        attn.reshape(rows, -1),
        grad_q.astype(jnp.bfloat16).reshape(rows, -1),
        key_gradient.reshape(length_total, -1),
        value_gradient.reshape(length_total, -1),
    )


def attend(query_rows, keys_in, values_in, grads_in, lengths_all, tiles_all, first_id, second_id):
    seq_ids = jnp.stack([first_id, second_id])
    lengths_pair = jnp.take(lengths_all, seq_ids, axis=0)
    tiles_pair = jnp.take(tiles_all, seq_ids, axis=0)
    ctx_rank = lax.axis_index("ctx")
    seq_dev = query_rows.shape[1]
    keys_all, values_all = (
        lax.all_gather(keys_in, "ctx", axis=1, tiled=True),
        lax.all_gather(values_in, "ctx", axis=1, tiled=True),
    )
    pieces = [
        sequence_core(
            query_rows[seq_slot],
            keys_all[seq_slot],
            values_all[seq_slot],
            grads_in[seq_slot],
            lengths_pair[seq_slot],
            tiles_pair[seq_slot],
            ctx_rank * seq_dev,
        )
        for seq_slot in range(2)
    ]
    attn = jnp.stack([pieces[0][0], pieces[1][0]])
    grad_q = jnp.stack([pieces[0][1], pieces[1][1]])
    key_terms = jnp.stack([pieces[0][2], pieces[1][2]])
    value_terms = jnp.stack([pieces[0][3], pieces[1][3]])
    key_sums, value_sums = (
        lax.psum_scatter(key_terms, "ctx", scatter_dimension=1, tiled=True),
        lax.psum_scatter(value_terms, "ctx", scatter_dimension=1, tiled=True),
    )
    return (attn, grad_q, key_sums.astype(jnp.bfloat16), value_sums.astype(jnp.bfloat16))


def take_second(mine, arrived, swapped):
    return jnp.stack([mine[0], jnp.where(swapped, arrived, mine[1])])


def shards(query_proj, key_proj, value_proj, grad_attn, doc_lengths, mask_tiles, pair_flags):
    dp_size = lax.axis_size("dp")
    dp_rank = lax.axis_index("dp")
    far_bit = dp_size.bit_length() - 2
    partner = jnp.bitwise_xor(dp_rank, dp_size // 2)
    pair_flag = lax.dynamic_index_in_dim(pair_flags, dp_rank, 0, keepdims=False)
    swapped = pair_flag == 1
    first_id = 2 * dp_rank
    second_id = jnp.where(swapped, 2 * partner + 1, 2 * dp_rank + 1)
    arrived = from_partner((query_proj[1], key_proj[1], value_proj[1], grad_attn[1]), "dp", far_bit)
    query_now = take_second(query_proj, arrived[0], swapped)
    key_now = take_second(key_proj, arrived[1], swapped)
    value_now = take_second(value_proj, arrived[2], swapped)
    grad_now = take_second(grad_attn, arrived[3], swapped)
    return attend(
        query_now, key_now, value_now, grad_now, doc_lengths, mask_tiles, first_id, second_id
    )


def solution(mesh):
    in_specs = (
        P("dp", "ctx", None),
        P("dp", "ctx", None),
        P("dp", "ctx", None),
        P("dp", "ctx", None),
        P(),
        P(),
        P(),
    )
    out_specs = (
        P("dp", "ctx", None),
        P("dp", "ctx", None),
        P("dp", "ctx", None),
        P("dp", "ctx", None),
    )
    return jax.shard_map(shards, mesh=mesh, in_specs=in_specs, out_specs=out_specs, check_vma=False)
```

profile of v0, /device:TPU:2, one launch (start us, length us, event | category | flops | bytes accessed | tf_op | source)
XLA Modules:
  0.0 379.0 jit_solution(14901232772893351566)
XLA Ops:
  14.0 2.4 collective-permute-done
  18.5 2.2 fusion.67
  31.9 4.0 %collective-permute-done.2 = bf16[64,4096]{1,0:T(8,128)(2,1)} collective-permute-done((bf16[64,4096]{1,0:T(8,128)(2,1)}, bf16[64,4096]{1,0:T(8,128)(2,1)}, u32[]{:S(2)}, u32[]{:S(2)}) %collective-permute-start.2) | collective-permute-done | bytes 524320 | tf_op jit(solution)/shard_map/ppermute | solution.py:14
  38.1 9.8 %collective-permute-done.3 = bf16[64,4096]{1,0:T(8,128)(2,1)} collective-permute-done((bf16[64,4096]{1,0:T(8,128)(2,1)}, bf16[64,4096]{1,0:T(8,128)(2,1)}, u32[]{:S(2)}, u32[]{:S(2)}) %collective-permute-start.3) | collective-permute-done | bytes 524320 | tf_op jit(solution)/shard_map/ppermute | solution.py:14
  50.2 33.2 %all-gather.3.cloned.1.call-done = bf16[2,512,1024]{2,0,1:T(2,128)(2,1)} async-done(((bf16[2,64,1024]{2,0,1:T(2,128)(2,1)}), bf16[2,512,1024]{2,0,1:T(2,128)(2,1)}) %all-gather.3.cloned.1.call-update) | async-done | bytes 2097168 | tf_op jit(solution)/shard_map/all_gather | solution.py:91
  83.4 6.6 %fusion.65 = (bf16[1,512,1024]{2,0,1:T(2,128)(2,1)}, bf16[1,512,1024]{2,0,1:T(2,128)(2,1)S(1)}) fusion(bf16[2,512,1024]{2,0,1:T(2,128)(2,1)} %all-gather.3.cloned.1.call-done), kind=kLoop, calls=%fused_computation.121 | loop fusion | bytes 4194304 | tf_op jit(solution)/shard_map/slice | solution.py:97
  90.0 5.8 %copy.180 = bf16[1,512,1024]{1,2,0:T(8,128)(2,1)} copy(bf16[1,512,1024]{2,0,1:T(2,128)(2,1)} %get-tuple-element.8) | data formatting | bytes 2097152
  95.8 4.2 %copy.182 = bf16[1,512,1024]{1,2,0:T(8,128)(2,1)} copy(bf16[1,512,1024]{2,0,1:T(2,128)(2,1)S(1)} %get-tuple-element.9) | data formatting | bytes 2097152
  100.0 45.6 %all-gather.5.cloned.1.call-done = bf16[2,512,1024]{2,0,1:T(2,128)(2,1)} async-done(((bf16[2,64,1024]{2,0,1:T(2,128)(2,1)}), bf16[2,512,1024]{2,0,1:T(2,128)(2,1)}) %all-gather.5.cloned.1.call-update) | async-done | bytes 2097168 | tf_op jit(solution)/shard_map/all_gather | solution.py:90
  145.6 6.5 %fusion.64 = (bf16[1,512,1024]{2,0,1:T(2,128)(2,1)S(1)}, bf16[1,512,1024]{2,0,1:T(2,128)(2,1)}) fusion(bf16[2,512,1024]{2,0,1:T(2,128)(2,1)} %all-gather.5.cloned.1.call-done), kind=kLoop, calls=%fused_computation.120 | loop fusion | bytes 4194304 | tf_op jit(solution)/shard_map/slice | solution.py:96
  152.1 2.6 copy.181
  154.7 4.6 %copy.183 = bf16[1,512,1024]{1,2,0:T(8,128)(2,1)S(1)} copy(bf16[1,512,1024]{2,0,1:T(2,128)(2,1)} %get-tuple-element.7) | data formatting | bytes 2097152
  161.0 2.1 fusion.70
  167.3 2.0 fusion.28
  169.3 2.9 copy.147
  172.9 2.1 fusion.71
  179.2 2.1 fusion.32
  181.3 2.9 copy.146
  184.1 4.7 %pad_maximum_fusion = f32[2,512,1024]{2,1,0:T(8,128)} fusion(f32[1,512,1024]{2,1,0:T(8,128)} %copy.147, f32[1,512,1024]{2,1,0:T(8,128)} %copy.146), kind=kLoop, calls=%fused_computation.4 | loop fusion | flops 1048576 | bytes 8388608 | tf_op jit(solution)/shard_map/stack | solution.py:107
  189.9 3.5 fusion.36
  193.4 2.9 copy.151
  196.3 3.5 fusion.39
  199.8 3.0 copy.150
  202.8 4.8 %pad_maximum_fusion.1 = f32[2,512,1024]{2,1,0:T(8,128)} fusion(f32[1,512,1024]{2,1,0:T(8,128)} %copy.151, f32[1,512,1024]{2,1,0:T(8,128)} %copy.150), kind=kLoop, calls=%fused_computation.5 | loop fusion | flops 1048576 | bytes 8388608 | tf_op jit(solution)/shard_map/stack | solution.py:108
  207.6 2.3 fusion.21
  211.1 2.3 stack_reshape.27
  213.4 2.2 copy.133
  215.6 2.3 stack_reshape.25
  223.4 54.4 %reduce-scatter.3.cloned.1.call-done = f32[2,64,1024]{2,1,0:T(8,128)} async-done(((f32[2,512,1024]{2,1,0:T(8,128)}), f32[2,64,1024]{2,1,0:T(8,128)}) %reduce-scatter.3.cloned.1.call-update) | async-done | bytes 524304 | tf_op jit(solution)/shard_map/reduce_scatter | solution.py:110
  277.8 1.8 convert_element_type.106
  279.6 91.1 %reduce-scatter.5.cloned.1.call-done = f32[2,64,1024]{2,1,0:T(8,128)} async-done(((f32[2,512,1024]{2,1,0:T(8,128)}), f32[2,64,1024]{2,1,0:T(8,128)}) %reduce-scatter.5.cloned.1.call-update) | async-done | bytes 524304 | tf_op jit(solution)/shard_map/reduce_scatter | solution.py:111
  370.7 1.8 convert_element_type.107
  (102 shorter events, 42.3 us)
Async XLA Ops:
  7.2 15.1 %copy-start.8 = (bf16[2,64,4096]{2,1,0:T(8,128)(2,1)S(1)}, bf16[2,64,4096]{2,1,0:T(8,128)(2,1)}, u32[]{:S(2)}) copy-start(bf16[2,64,4096]{2,1,0:T(8,128)(2,1)} %param.10) | copy-start | bytes 3145732
  7.2 16.4 %copy-start.17 = (s32[64,8]{0,1:T(8,128)S(1)}, s32[64,8]{0,1:T(8,128)}, u32[]{:S(2)}) copy-start(s32[64,8]{0,1:T(8,128)} %param.11) | copy-start | bytes 6148
  7.2 17.7 %copy-start.16 = (s32[64,8,8]{0,2,1:T(8,128)S(1)}, s32[64,8,8]{0,2,1:T(8,128)}, u32[]{:S(2)}) copy-start(s32[64,8,8]{0,2,1:T(8,128)} %param.12) | copy-start | bytes 49156
  7.2 76.2 %all-gather.3.cloned.1.call-start = ((), (), s32[]{:S(2)}) async-start(), calls=%async_computation.2 | async-start | bytes 2359296 | tf_op jit(solution)/shard_map/all_gather | solution.py:91
  8.3 5.7 %collective-permute-start.1 = (bf16[64,1024]{1,0:T(8,128)(2,1)S(1)}, bf16[64,1024]{1,0:T(8,128)(2,1)S(1)}, u32[]{:S(2)}, u32[]{:S(2)}) collective-permute-start(bf16[64,1024]{1,0:T(8,128)(2,1)S(1)} %get-tuple-element.15), channel_id=1, source_target_pairs={{0,128},{8,136},{16,144},{24,152},{32,160},{40,168},{48,176},{56,1... | collective-permute-start | bytes 393224 | tf_op jit(solution)/shard_map/ppermute | solution.py:14
  11.0 5.5 %collective-permute-start = (bf16[64,1024]{1,0:T(8,128)(2,1)S(1)}, bf16[64,1024]{1,0:T(8,128)(2,1)S(1)}, u32[]{:S(2)}, u32[]{:S(2)}) collective-permute-start(bf16[64,1024]{1,0:T(8,128)(2,1)S(1)} %get-tuple-element.17), channel_id=1, source_target_pairs={{0,128},{8,136},{16,144},{24,152},{32,160},{40,168},{48,176},{56,1... | collective-permute-start | bytes 393224 | tf_op jit(solution)/shard_map/ppermute | solution.py:14
  18.5 17.4 %copy-start.7 = (bf16[2,64,4096]{2,1,0:T(8,128)(2,1)S(1)}, bf16[2,64,4096]{2,1,0:T(8,128)(2,1)}, u32[]{:S(2)}) copy-start(bf16[2,64,4096]{2,1,0:T(8,128)(2,1)} %param.7) | copy-start | bytes 3145732
  18.5 127.1 %all-gather.5.cloned.1.call-start = ((), (), s32[]{:S(2)}) async-start(), calls=%async_computation.3 | async-start | bytes 2359296 | tf_op jit(solution)/shard_map/all_gather | solution.py:90
  20.7 15.2 %collective-permute-start.2 = (bf16[64,4096]{1,0:T(8,128)(2,1)}, bf16[64,4096]{1,0:T(8,128)(2,1)}, u32[]{:S(2)}, u32[]{:S(2)}) collective-permute-start(bf16[64,4096]{1,0:T(8,128)(2,1)} %get-tuple-element.13), channel_id=1, source_target_pairs={{0,128},{8,136},{16,144},{24,152},{32,160},{40,168},{48,176},{56,1... | collective-permute-start | bytes 1572872 | tf_op jit(solution)/shard_map/ppermute | solution.py:14
  23.1 24.8 %collective-permute-start.3 = (bf16[64,4096]{1,0:T(8,128)(2,1)}, bf16[64,4096]{1,0:T(8,128)(2,1)}, u32[]{:S(2)}, u32[]{:S(2)}) collective-permute-start(bf16[64,4096]{1,0:T(8,128)(2,1)} %get-tuple-element.11), channel_id=1, source_target_pairs={{0,128},{8,136},{16,144},{24,152},{32,160},{40,168},{48,176},{56,1... | collective-permute-start | bytes 1572872 | tf_op jit(solution)/shard_map/ppermute | solution.py:14
  30.8 247.1 %reduce-scatter.3.cloned.1.call-start = ((), (), s32[]{:S(2)}) async-start(), calls=%async_computation.4 | async-start | bytes 4718592 | tf_op jit(solution)/shard_map/reduce_scatter | solution.py:110
  163.1 1.0 copy-start.10
  163.1 1.5 copy-start.15
  163.5 3.8 copy-start
  166.1 1.1 copy-start.6
  167.3 2.0 copy-start.2
  167.3 4.9 %copy-start.5 = (bf16[64,8,4,128]{3,2,1,0:T(4,128)(2,1)S(1)}, bf16[64,8,4,128]{3,2,1,0:T(4,128)(2,1)}, u32[]{:S(2)}) copy-start(bf16[64,8,4,128]{3,2,1,0:T(4,128)(2,1)} %reshape_squeeze_stack_squeeze.6) | copy-start | bytes 1572868
  175.0 1.0 copy-start.9
  175.0 1.5 copy-start.14
  175.4 3.8 copy-start.1
  179.2 2.1 copy-start.3
  188.9 1.0 copy-start.11
  188.9 181.8 %reduce-scatter.5.cloned.1.call-start = ((), (), s32[]{:S(2)}) async-start(), calls=%async_computation.5 | async-start | bytes 4718592 | tf_op jit(solution)/shard_map/reduce_scatter | solution.py:111
  209.9 8.0 %copy-start.4 = (bf16[8,4,64,512]{3,2,1,0:T(8,128)(2,1)S(1)}, bf16[8,4,64,512]{3,2,1,0:T(8,128)(2,1)}, u32[]{:S(2)}) copy-start(bf16[8,4,64,512]{3,2,1,0:T(8,128)(2,1)} %copy-done.3) | copy-start | bytes 6291460
  218.6 2.7 copy-start.12
  218.6 3.7 copy-start.13
Sparse Core Ops, SparseCore 0:
  18.6 64.7 all-gather.2
  86.6 58.9 all-gather.4
  189.0 88.7 reduce-scatter.2
  281.9 88.7 reduce-scatter.4
where the time goes:
time: 380 us; the launch traced here: 379 us
  waiting for transfers between devices  241 us (63%)
  local copies, waits for them, and re-layouts  71.7 us (19%)
  other arithmetic  24.4 us (6%)
  matrix products  22.5 us (6%)
  between operations  14.8 us (4%)
  starting transfers between devices  4.39 us (1%)
    reduce_scatter x1, waiting for transfers between devices, attend(): lax.psum_scatter(value_terms, 'ctx', scatter_dimension=1, tiled=True)  91.1 us
    reduce_scatter x1, waiting for transfers between devices, attend(): lax.psum_scatter(key_terms, 'ctx', scatter_dimension=1, tiled=True)  54.4 us
    all_gather x1, waiting for transfers between devices, attend(): lax.all_gather(keys_in, 'ctx', axis=1, tiled=True)  45.6 us
    all_gather x1, waiting for transfers between devices, attend(): lax.all_gather(values_in, 'ctx', axis=1, tiled=True)  33.2 us
    unnamed x42, local copies, waits for them, and re-layouts  21.4 us
    ppermute x4, waiting for transfers between devices, from_partner(): return lax.ppermute(value, axis, pairs)  16.9 us
  transfers between devices with their start and end apart: 8, of which 8 were waited for; matrix products, arithmetic and copies ran while one was open for 18% of the time, Pallas kernels for 0%

commit v1 on v0

--- a/solution.py
+++ b/solution.py
@@ -87,7 +87,9 @@
     ctx_rank = lax.axis_index("ctx")
     seq_dev = query_rows.shape[1]
     keys_all, values_all = (
-        lax.all_gather(keys_in, "ctx", axis=1, tiled=True),
+        jnp.concatenate(
+            lax.all_to_all(jnp.stack([keys_in] * lax.axis_size("ctx")), "ctx", 0, 0), axis=1
+        ),
         lax.all_gather(values_in, "ctx", axis=1, tiled=True),
     )
     pieces = [

time: 380 us -> 300 us (0.79)
  waiting for transfers between devices: 241 us -> 163 us
  local copies, waits for them, and re-layouts: 71.7 us -> 57 us
  starting transfers between devices: 4.39 us -> 11.9 us
  matrix products: 22.5 us -> 27.8 us
    reduce_scatter x1, waiting for transfers between devices: 91.1 us -> 34.1 us  [attend(): lax.psum_scatter(value_terms, 'ctx', scatter_dimension=1, tiled=True)]
    all_gather x1 -> x0, waiting for transfers between devices: 45.6 us -> none  [attend(): lax.all_gather(keys_in, 'ctx', axis=1, tiled=True)]
    reduce_scatter x1, waiting for transfers between devices: 54.4 us -> 91.2 us  [attend(): lax.psum_scatter(key_terms, 'ctx', scatter_dimension=1, tiled=True)]
    all_to_all x0 -> x1, waiting for transfers between devices: none -> 20.9 us  [attend(): lax.all_to_all(jnp.stack([keys_in] * lax.axis_size('ctx')), 'ctx', 0, 0)]
    all_gather x1, waiting for transfers between devices: 33.2 us -> 13.8 us  [attend(): lax.all_gather(values_in, 'ctx', axis=1, tiled=True)]
    ppermute x4, waiting for transfers between devices: 16.9 us -> 2.53 us  [from_partner(): return lax.ppermute(value, axis, pairs)]
    all_to_all x0 -> x1, starting transfers between devices: none -> 7.46 us  [attend(): lax.all_to_all(jnp.stack([keys_in] * lax.axis_size('ctx')), 'ctx', 0, 0)]
    slice x1, local copies, waits for them, and re-layouts: 6.49 us -> 0.17 us  [attend(): keys_all[seq_slot]]
  transfers between devices with their start and end apart: 8 -> 8, of which waited for: 8 -> 5; matrix products, arithmetic and copies ran while one was open for 18% -> 34% of each run, Pallas kernels for 0% -> 0%
where the time goes in v1:
time: 300 us; the launch traced here: 299 us
  waiting for transfers between devices  163 us (54%)
  local copies, waits for them, and re-layouts  57 us (19%)
  matrix products  27.8 us (9%)
  other arithmetic  25.4 us (8%)
  between operations  14.8 us (5%)
  starting transfers between devices  11.9 us (4%)
    reduce_scatter x1, waiting for transfers between devices, attend(): lax.psum_scatter(key_terms, 'ctx', scatter_dimension=1, tiled=True)  91.2 us
    reduce_scatter x1, waiting for transfers between devices, attend(): lax.psum_scatter(value_terms, 'ctx', scatter_dimension=1, tiled=True)  34.1 us
    all_to_all x1, waiting for transfers between devices, attend(): lax.all_to_all(jnp.stack([keys_in] * lax.axis_size('ctx')), 'ctx', 0, 0)  20.9 us
    unnamed x44, local copies, waits for them, and re-layouts  17.8 us
    all_gather x1, waiting for transfers between devices, attend(): lax.all_gather(values_in, 'ctx', axis=1, tiled=True)  13.8 us
    all_to_all x1, starting transfers between devices, attend(): lax.all_to_all(jnp.stack([keys_in] * lax.axis_size('ctx')), 'ctx', 0, 0)  7.46 us
    dot_general x2, matrix products, sequence_core(): jnp.einsum('grij,jgd->igrd', probs_b, heads_of_values, preferred_element_...  7.32 us
    slice x1, local copies, waits for them, and re-layouts, attend(): values_all[seq_slot]  6.83 us
  transfers between devices with their start and end apart: 8, of which 5 were waited for; matrix products, arithmetic and copies ran while one was open for 34% of the time, Pallas kernels for 0%

profile of v1, /device:TPU:2, one launch (start us, length us, event | category | flops | bytes accessed | tf_op | source)
XLA Modules:
  0.0 299.3 jit_solution(4400337638112103070)
XLA Ops:
  12.0 2.1 fusion.71
  15.7 2.1 fusion.70
  28.2 7.5 %all-to-all-start = ((bf16[8,2,64,1024]{3,2,1,0:T(8,128)(2,1)}), bf16[8,2,64,1024]{3,2,1,0:T(8,128)(2,1)S(1)}, u32[]{:S(2)}, u32[]{:S(2)}) async-start(bf16[8,2,64,1024]{3,2,1,0:T(8,128)(2,1)} %stack.60), calls=%async_computation | async-start | bytes 4194304 | tf_op jit(solution)/shard_map/all_to_all | solution.py:91
  35.6 1.9 broadcast_select_fusion.1
  38.9 2.5 collective-permute-done.3
  41.5 2.1 broadcast_select_fusion
  43.6 2.2 reshape_squeeze_stack.7
  45.7 20.9 %all-to-all-done = bf16[8,2,64,1024]{3,2,1,0:T(8,128)(2,1)S(1)} async-done(((bf16[8,2,64,1024]{3,2,1,0:T(8,128)(2,1)}), bf16[8,2,64,1024]{3,2,1,0:T(8,128)(2,1)S(1)}, u32[]{:S(2)}, u32[]{:S(2)}) %all-to-all-start) | async-done | bytes 2097184 | tf_op jit(solution)/shard_map/all_to_all | solution.py:91
  68.1 2.1 fusion.74
  71.9 1.9 fusion.40
  73.8 2.9 copy.143
  77.5 2.1 fusion.75
  81.3 1.9 fusion.43
  83.2 2.9 copy.142
  86.2 4.7 %pad_maximum_fusion.1 = f32[2,512,1024]{2,1,0:T(8,128)} fusion(f32[1,512,1024]{2,1,0:T(8,128)} %copy.143, f32[1,512,1024]{2,1,0:T(8,128)} %copy.142), kind=kLoop, calls=%fused_computation.5 | loop fusion | flops 1048576 | bytes 8388608 | tf_op jit(solution)/shard_map/stack | solution.py:110
  91.2 13.8 %all-gather.2.cloned.1.call-done = bf16[2,512,1024]{2,0,1:T(2,128)(2,1)} async-done(((bf16[2,64,1024]{2,0,1:T(2,128)(2,1)}), bf16[2,512,1024]{2,0,1:T(2,128)(2,1)}) %all-gather.2.cloned.1.call-update) | async-done | bytes 2097168 | tf_op jit(solution)/shard_map/all_gather | solution.py:93
  105.0 6.8 %fusion.69 = (bf16[1,512,1024]{2,0,1:T(2,128)(2,1)}, bf16[1,512,1024]{2,0,1:T(2,128)(2,1)}) fusion(bf16[2,512,1024]{2,0,1:T(2,128)(2,1)} %all-gather.2.cloned.1.call-done), kind=kLoop, calls=%fused_computation.125 | loop fusion | bytes 4194304 | tf_op jit(solution)/shard_map/slice | solution.py:99
  111.8 5.8 %copy.172 = bf16[1,512,1024]{1,2,0:T(8,128)(2,1)} copy(bf16[1,512,1024]{2,0,1:T(2,128)(2,1)} %get-tuple-element.8) | data formatting | bytes 2097152
  117.7 5.8 %copy.173 = bf16[1,512,1024]{1,2,0:T(8,128)(2,1)} copy(bf16[1,512,1024]{2,0,1:T(2,128)(2,1)} %get-tuple-element.9) | data formatting | bytes 2097152
  123.5 3.6 %multiply_reduce_fusion = (f32[64,8,4]{0,2,1:T(4,128)S(1)}, bf16[64,8,4,128]{3,0,2,1:T(8,128)(2,1)}) fusion(bf16[64,8,4,128]{3,2,1,0:T(4,128)(2,1)} %reshape_squeeze_stack.7, bf16[512,8,128,1]{0,2,3,1:T(8,128)(2,1)} %bitcast.169, bf16[8,4,64,512]{3,2,1,0:T(8,128)(2,1)} %copy-done.1), kind=kOutput, calls=%fused_computation.46 | convolution fusion | flops 269744128 | bytes 4202496 | tf_op jit(solution)/shard_map/grij,jgd->igrd/dot_general | solution.py:56
  127.2 2.3 fusion.4
  130.8 1.9 fusion.34
  132.8 3.0 copy.139
  135.7 3.7 %multiply_reduce_fusion.1 = (f32[64,8,4]{0,2,1:T(4,128)S(1)}, bf16[64,8,4,128]{3,0,2,1:T(8,128)(2,1)}) fusion(bf16[64,8,4,128]{3,2,1,0:T(4,128)(2,1)S(1)} %copy-done.9, bf16[512,8,128,1]{0,2,3,1:T(8,128)(2,1)} %bitcast.167, bf16[8,4,64,512]{3,2,1,0:T(8,128)(2,1)} %copy-done), kind=kOutput, calls=%fused_computation.47 | convolution fusion | flops 269744128 | bytes 4202496 | tf_op jit(solution)/shard_map/grij,jgd->igrd/dot_general | solution.py:56
  139.4 2.3 fusion.7
  143.0 1.9 fusion.37
  144.9 2.9 copy.138
  147.8 4.9 %pad_maximum_fusion = f32[2,512,1024]{2,1,0:T(8,128)} fusion(f32[1,512,1024]{2,1,0:T(8,128)} %copy.139, f32[1,512,1024]{2,1,0:T(8,128)} %copy.138), kind=kLoop, calls=%fused_computation.4 | loop fusion | flops 1048576 | bytes 8388608 | tf_op jit(solution)/shard_map/stack | solution.py:109
  152.8 2.4 fusion.21
  156.8 2.3 fusion.20
  163.9 34.1 %reduce-scatter.5.cloned.1.call-done = f32[2,64,1024]{2,1,0:T(8,128)} async-done(((f32[2,512,1024]{2,1,0:T(8,128)}), f32[2,64,1024]{2,1,0:T(8,128)}) %reduce-scatter.5.cloned.1.call-update) | async-done | bytes 524304 | tf_op jit(solution)/shard_map/reduce_scatter | solution.py:113
  199.8 91.2 %reduce-scatter.3.cloned.1.call-done = f32[2,64,1024]{2,1,0:T(8,128)} async-done(((f32[2,512,1024]{2,1,0:T(8,128)}), f32[2,64,1024]{2,1,0:T(8,128)}) %reduce-scatter.3.cloned.1.call-update) | async-done | bytes 524304 | tf_op jit(solution)/shard_map/reduce_scatter | solution.py:112
  (103 shorter events, 35.9 us)
Async XLA Ops:
  7.2 11.1 %copy-start.16 = (s32[32]{0:T(128)S(1)}, s32[32]{0:T(128)}, u32[]{:S(2)}) copy-start(s32[32]{0:T(128)} %param.13) | copy-start | bytes 388
  7.2 12.4 %copy-start.15 = (s32[64,8]{0,1:T(8,128)S(1)}, s32[64,8]{0,1:T(8,128)}, u32[]{:S(2)}) copy-start(s32[64,8]{0,1:T(8,128)} %param.11) | copy-start | bytes 6148
  7.2 13.8 %copy-start.14 = (s32[64,8,8]{0,2,1:T(8,128)S(1)}, s32[64,8,8]{0,2,1:T(8,128)}, u32[]{:S(2)}) copy-start(s32[64,8,8]{0,2,1:T(8,128)} %param.12) | copy-start | bytes 49156
  7.2 97.8 %all-gather.2.cloned.1.call-start = ((), (), s32[]{:S(2)}) async-start(), calls=%async_computation.3 | async-start | bytes 2359296 | tf_op jit(solution)/shard_map/all_gather | solution.py:93
  8.2 17.2 %copy-start.11 = (bf16[2,64,1024]{2,1,0:T(8,128)(2,1)S(1)}, bf16[2,64,1024]{2,1,0:T(8,128)(2,1)}, u32[]{:S(2)}) copy-start(bf16[2,64,1024]{2,1,0:T(8,128)(2,1)} %param.8) | copy-start | bytes 786436
  8.2 17.2 %copy-start.12 = (bf16[2,64,1024]{2,1,0:T(8,128)(2,1)S(1)}, bf16[2,64,1024]{2,1,0:T(8,128)(2,1)}, u32[]{:S(2)}) copy-start(bf16[2,64,1024]{2,1,0:T(8,128)(2,1)} %param.9) | copy-start | bytes 786436
  8.3 17.2 %collective-permute-start.1 = (bf16[64,1024]{1,0:T(8,128)(2,1)S(1)}, bf16[64,1024]{1,0:T(8,128)(2,1)S(1)}, u32[]{:S(2)}, u32[]{:S(2)}) collective-permute-start(bf16[64,1024]{1,0:T(8,128)(2,1)S(1)} %get-tuple-element.15), channel_id=1, source_target_pairs={{0,128},{8,136},{16,144},{24,152},{32,160},{40,168},{48,176},{56,1... | collective-permute-start | bytes 393224 | tf_op jit(solution)/shard_map/ppermute | solution.py:14
  11.6 13.9 %collective-permute-start = (bf16[64,1024]{1,0:T(8,128)(2,1)}, bf16[64,1024]{1,0:T(8,128)(2,1)S(1)}, u32[]{:S(2)}, u32[]{:S(2)}) collective-permute-start(bf16[64,1024]{1,0:T(8,128)(2,1)} %get-tuple-element.17), channel_id=1, source_target_pairs={{0,128},{8,136},{16,144},{24,152},{32,160},{40,168},{48,176},{56,1... | collective-permute-start | bytes 393224 | tf_op jit(solution)/shard_map/ppermute | solution.py:14
  14.1 21.5 %collective-permute-start.2 = (bf16[64,4096]{1,0:T(8,128)(2,1)}, bf16[64,4096]{1,0:T(8,128)(2,1)S(1)}, u32[]{:S(2)}, u32[]{:S(2)}) collective-permute-start(bf16[64,4096]{1,0:T(8,128)(2,1)} %get-tuple-element.13), channel_id=1, source_target_pairs={{0,128},{8,136},{16,144},{24,152},{32,160},{40,168},{48,176},{56,1... | collective-permute-start | bytes 1572872 | tf_op jit(solution)/shard_map/ppermute | solution.py:14
  17.8 23.7 %collective-permute-start.3 = (bf16[64,4096]{1,0:T(8,128)(2,1)}, bf16[64,4096]{1,0:T(8,128)(2,1)}, u32[]{:S(2)}, u32[]{:S(2)}) collective-permute-start(bf16[64,4096]{1,0:T(8,128)(2,1)} %get-tuple-element.11), channel_id=1, source_target_pairs={{0,128},{8,136},{16,144},{24,152},{32,160},{40,168},{48,176},{56,1... | collective-permute-start | bytes 1572872 | tf_op jit(solution)/shard_map/ppermute | solution.py:14
  28.2 38.4 %all-to-all-start = ((bf16[8,2,64,1024]{3,2,1,0:T(8,128)(2,1)}), bf16[8,2,64,1024]{3,2,1,0:T(8,128)(2,1)S(1)}, u32[]{:S(2)}, u32[]{:S(2)}) async-start(bf16[8,2,64,1024]{3,2,1,0:T(8,128)(2,1)} %stack.60), calls=%async_computation | async-start | bytes 4194304 | tf_op jit(solution)/shard_map/all_to_all | solution.py:91
  35.6 162.4 %reduce-scatter.5.cloned.1.call-start = ((), (), s32[]{:S(2)}) async-start(), calls=%async_computation.5 | async-start | bytes 4718592 | tf_op jit(solution)/shard_map/reduce_scatter | solution.py:113
  67.0 1.0 copy-start.18
  70.2 3.6 %copy-start.6 = (f32[8,4,64,512]{3,2,1,0:T(8,128)}, f32[8,4,64,512]{3,2,1,0:T(8,128)S(1)}, u32[]{:S(2)}) copy-start(f32[8,4,64,512]{3,2,1,0:T(8,128)S(1)} %get-tuple-element.21) | copy-start | bytes 12582916
  70.2 1.7 copy-start.10
  70.6 1.3 copy-start.1
  73.8 3.6 %copy-start.17 = (pred[64,512]{1,0:T(8,128)(4,1)S(1)}, pred[64,512]{1,0:T(8,128)(4,1)}, u32[]{:S(2)}) copy-start(pred[64,512]{1,0:T(8,128)(4,1)} %fusion.22) | copy-start | bytes 98308
  79.6 3.6 %copy-start.4 = (f32[8,4,64,512]{3,2,1,0:T(8,128)}, f32[8,4,64,512]{3,2,1,0:T(8,128)S(1)}, u32[]{:S(2)}) copy-start(f32[8,4,64,512]{3,2,1,0:T(8,128)S(1)} %get-tuple-element.23) | copy-start | bytes 12582916
  79.6 1.7 copy-start.8
  80.0 1.3 copy-start
  90.9 200.0 %reduce-scatter.3.cloned.1.call-start = ((), (), s32[]{:S(2)}) async-start(), calls=%async_computation.4 | async-start | bytes 4718592 | tf_op jit(solution)/shard_map/reduce_scatter | solution.py:112
  123.5 3.7 %copy-start.7 = (f32[8,4,64,512]{3,2,1,0:T(8,128)S(1)}, f32[8,4,64,512]{3,2,1,0:T(8,128)}, u32[]{:S(2)}) copy-start(f32[8,4,64,512]{3,2,1,0:T(8,128)} %copy-done.6) | copy-start | bytes 12582916
  129.5 1.4 copy-start.2
  132.8 3.0 copy-start.9
  135.7 3.7 %copy-start.5 = (f32[8,4,64,512]{3,2,1,0:T(8,128)S(1)}, f32[8,4,64,512]{3,2,1,0:T(8,128)}, u32[]{:S(2)}) copy-start(f32[8,4,64,512]{3,2,1,0:T(8,128)} %copy-done.4) | copy-start | bytes 12582916
  141.7 1.3 copy-start.3
  152.8 3.2 %copy-start.13 = (bf16[64,8,4,128]{3,0,2,1:T(8,128)(2,1)S(1)}, bf16[64,8,4,128]{3,0,2,1:T(8,128)(2,1)}, u32[]{:S(2)}) copy-start(bf16[64,8,4,128]{3,0,2,1:T(8,128)(2,1)} %get-tuple-element.25) | copy-start | bytes 1572868
Sparse Core Ops, SparseCore 0:
  26.6 78.3 all-gather.1
  109.2 88.7 reduce-scatter.4
  202.2 88.7 reduce-scatter.2
